TPU v7x, 32 devices: a whole 2x2x4 slice. The times are simulated.
32 devices in a mesh: gx: 16 (over z, y, x), gy: 2 (over core).
Axes of the slice: x: 2, y: 2, z: 4, core: 2. Of those that a mesh axis runs over, the one named last changes fastest.
Arguments:
- features: bfloat16 [16, 2, 2, 512, 128], P('gx', 'gy'), may hold values from -6 to 6
- cotangent: bfloat16 [16, 2, 2, 512, 128], P('gx', 'gy'), may hold values from -6 to 6
- neighbours: int32 [16, 2, 2, 27], P('gx', 'gy'), may hold values from -1 to 17, as said below
- weights: bfloat16 [27, 128, 128], replicated, may hold values from -0.109375 to 0.109375
- channel_gain: float32 [128], replicated, may hold values from 0.5 to 2
Outputs:
- output: bfloat16 [16, 2, 2, 512, 128], P('gx', 'gy')
- input_grad: bfloat16 [16, 2, 2, 512, 128], P('gx', 'gy')
- weight_grad: float32 [27, 128, 128], replicated
- gain_grad: float32 [128], replicated
Inputs may be any that keep to these rules, and one draw needn't show every extreme that they name: `neighbours`: entry [i, j, s, k] names, for slot s of device (i, j) and direction k = 9 (a + 1) + 3 (b + 1) + (c + 1), the block at block offset (a, b, c): the code (3 (i2 - i + 1) + (j2 - j + 1)) * 2 + s2 for slot s2 of device (i2, j2), always equal or beside (i, j), with i2 - i equal to 0 or a and j2 - j equal to 0 or b, or -1 where no occupied block lies. Codes are therefore at most 17. Entry 13 is 8 + s for an occupied slot; an empty slot has -1 everywhere. The relation is symmetric: the block named in direction k names the first one back in direction 26 - k. Some device has all 2 slots occupied.
All inputs are finite; a program needn't handle non-finite values.
Results may differ from a plain program's by a relative error of at most 0.0042.
Values may be sent and summed in bfloat16 or wider, within the bound.
A program may use at most 64 MiB of HBM per device.

v0:
```python
from functools import partial

import jax
import jax.numpy as jnp
from jax import lax
from jax.sharding import PartitionSpec as P

DIRECTIONS = [(a, b, c) for a in (-1, 0, 1) for b in (-1, 0, 1) for c in (-1, 0, 1)]


def padded(value, sides, width):
    for axis, dim in sides:
        count, length = (lax.axis_size(axis), value.shape[dim])
        up = [(i, (i + 1) % count) for i in range(count - 1)]
        down = [(j, i) for i, j in up]
        last = lax.slice_in_dim(value, length - width, length, axis=dim)
        leading = lax.slice_in_dim(value, 0, width, axis=dim)
        before = lax.ppermute(last, axis, up)
        after = lax.ppermute(leading, axis, down)
        value = jnp.concatenate([before, value, after], axis=dim)
    return value


def rim_bounds(d):
    if d < 0:
        return (7, 8)
    if d == 0:
        return (0, 8)
    return (0, 1)


def rim_range(d):
    lower, upper = rim_bounds(d)
    return slice(lower, upper)


def region_of(gathered_table, use_faces, a, b, c):
    return gathered_table[:, rim_range(a), rim_range(b), rim_range(c)]


def assemble(own_blocks, region_fn, slot_codes):
    planes = []
    for a in (-1, 0, 1):
        row_parts = []
        for b in (-1, 0, 1):
            col_parts = []
            for c in (-1, 0, 1):
                k = (a + 1) * 9 + (b + 1) * 3 + (c + 1)
                if k == 13:
                    block_piece = own_blocks
                else:
                    region = region_fn(a, b, c)
                    block_piece = jnp.take(region, jnp.maximum(slot_codes[:, k], 0), axis=0)
                    present = (slot_codes[:, k] >= 0)[:, None, None, None, None]
                    block_piece = jnp.where(present, block_piece, jnp.zeros((), block_piece.dtype))
                col_parts.append(block_piece)
            row_parts.append(jnp.concatenate(col_parts, axis=3))
        planes.append(jnp.concatenate(row_parts, axis=2))
    return jnp.concatenate(planes, axis=1)


def window(padded_tile, a, b, c):
    capacity = padded_tile.shape[0]
    channels = padded_tile.shape[-1]
    return padded_tile[:, 1 + a : 9 + a, 1 + b : 9 + b, 1 + c : 9 + c].reshape(
        capacity * 512, channels
    )


def convolve(padded_tile, weights):
    total = None
    for k in range(27):
        a, b, c = DIRECTIONS[k]
        term = jnp.dot(window(padded_tile, a, b, c), weights[k], preferred_element_type=jnp.float32)
        total = term if total is None else total + term
    return total


def convolve_adjoint(padded_tile, weights):
    total = None
    for k in range(27):
        a, b, c = DIRECTIONS[k]
        term = lax.dot_general(
            window(padded_tile, -a, -b, -c),
            weights[k],
            (((1,), (1,)), ((), ())),
            preferred_element_type=jnp.float32,
        )
        total = term if total is None else total + term
    return total


def weight_terms(padded_tile, scaled):
    terms = []
    for k in range(27):
        a, b, c = DIRECTIONS[k]
        terms.append(
            lax.dot_general(
                window(padded_tile, a, b, c),
                scaled,
                (((0,), (0,)), ((), ())),
                preferred_element_type=jnp.float32,
            )
        )
    return jnp.stack(terms, axis=0)


def forward_table(own_blocks):
    capacity = own_blocks.shape[0]
    channels = own_blocks.shape[-1]
    sent = own_blocks.reshape(1, 1, capacity, 512, channels)
    received = padded(sent, (("gx", 0), ("gy", 1)), 1)
    return partial(region_of, received.reshape(9 * capacity, 8, 8, 8, channels), False)


def backward_table(own_blocks):
    capacity = own_blocks.shape[0]
    channels = own_blocks.shape[-1]
    sent = own_blocks.reshape(1, 1, capacity, 512, channels)
    received = padded(sent, (("gx", 0), ("gy", 1)), 1)
    return partial(region_of, received.reshape(9 * capacity, 8, 8, 8, channels), False)


def on_device(features, cotangent, neighbours, weights, channel_gain):
    slot_codes = neighbours[0, 0]
    capacity = features.shape[2]
    channels = features.shape[-1]
    occupied = (slot_codes[:, 13] >= 0)[:, None, None]
    own_x = jnp.where(occupied, features[0, 0], jnp.zeros((), features.dtype)).reshape(
        capacity, 8, 8, 8, channels
    )
    regions_x = forward_table(own_x)
    tile_x = assemble(own_x, regions_x, slot_codes)
    conv_out = convolve(tile_x, weights)
    pre_act = own_x.reshape(-1, channels).astype(jnp.float32) + channel_gain * conv_out
    sigmoid_value = jax.nn.sigmoid(pre_act)
    result = (pre_act * sigmoid_value).astype(jnp.bfloat16)
    upstream = (
        jnp.where(occupied, cotangent[0, 0], jnp.zeros((), cotangent.dtype))
        .reshape(-1, channels)
        .astype(jnp.float32)
    )
    pre_grad = upstream * sigmoid_value * (1.0 + pre_act * (1.0 - sigmoid_value))
    scaled = (channel_gain * pre_grad).astype(jnp.bfloat16)
    own_u = scaled.reshape(capacity, 8, 8, 8, channels)
    regions_u = backward_table(own_u)
    tile_u = assemble(own_u, regions_u, slot_codes)
    grad_here = (pre_grad + convolve_adjoint(tile_u, weights)).astype(jnp.bfloat16)
    local_weight = weight_terms(tile_x, scaled)
    local_gain = jnp.sum(pre_grad * conv_out, axis=0)
    weight_grad, gain_grad = lax.psum((local_weight, local_gain), ("gx", "gy"))
    return (
        result.reshape(1, 1, capacity, 512, channels),
        grad_here.reshape(1, 1, capacity, 512, channels),
        weight_grad,
        gain_grad,
    )


def solution(mesh):
    in_specs = (
        P("gx", "gy", None, None, None),
        P("gx", "gy", None, None, None),
        P("gx", "gy", None, None),
        P(),
        P(),
    )
    out_specs = (P("gx", "gy", None, None, None), P("gx", "gy", None, None, None), P(), P())
    return jax.shard_map(
        on_device, mesh=mesh, in_specs=in_specs, out_specs=out_specs, check_vma=False
    )
```

profile of v0, /device:TPU:0, one launch (start us, length us, event | category | flops | bytes accessed | tf_op | source)
XLA Modules:
  0.0 304.9 jit_solution(12972801754330378274)
XLA Ops:
  7.2 1.8 compare_reduce_fusion.25
  10.1 4.9 %collective-permute-start = (bf16[1,1,2,512,128]{4,3,2,1,0:T(8,128)(2,1)S(1)}, bf16[1,1,2,512,128]{4,3,2,1,0:T(8,128)(2,1)S(1)}, u32[]{:S(2)}, u32[]{:S(2)}) collective-permute-start(bf16[1,1,2,512,128]{4,3,2,1,0:T(8,128)(2,1)S(1)} %broadcast_select_fusion.1), channel_id=1, source_target_pairs={{0,2},{2,4},{4,6},{6,8},{8,10},{10,12},{12,14},{14,16},{16,18},{18... | collective-permute-start | bytes 786440 | tf_op jit(solution)/shard_map/ppermute | solution.py:18
  15.0 1.3 collective-permute-start.1
  16.3 1.9 maximum_reduce_fusion.8
  18.2 2.5 compare_reduce_fusion.8
  30.7 1.2 maximum_reduce_fusion.6
  48.6 1.5 collective-permute-start.2
  50.1 1.5 collective-permute-start.3
  55.0 1.2 fusion.182
  69.3 1.2 gather_fusion.8
  79.8 1.5 copy.266
  81.3 1.4 gather_fusion.3
  84.1 1.4 gather_fusion.5
  97.2 1.4 gather_fusion.7
  98.6 1.4 gather_fusion.1
  100.1 1.6 gather_fusion.4
  101.7 1.5 gather_fusion.18
  122.6 4.4 %collective-permute-start.4 = (bf16[1,1,2,512,128]{4,3,2,1,0:T(8,128)(2,1)S(1)}, bf16[1,1,2,512,128]{4,3,2,1,0:T(8,128)(2,1)S(1)}, u32[]{:S(2)}, u32[]{:S(2)}) collective-permute-start(bf16[1,1,2,512,128]{4,3,2,1,0:T(8,128)(2,1)S(1)} %bitcast.836), channel_id=1, source_target_pairs={{0,2},{2,4},{4,6},{6,8},{8,10},{10,12},{12,14},{14,16},{16,18},{18... | collective-permute-start | bytes 786440 | tf_op jit(solution)/shard_map/ppermute | solution.py:18
  127.0 1.5 collective-permute-start.5
  149.3 2.0 collective-permute-start.6
  151.3 1.3 collective-permute-start.7
  156.2 44.2 %psum.15 = f32[128]{0:T(128)} all-reduce(f32[128]{0:T(128)S(1)} %get-tuple-element.64), channel_id=1, replica_groups=mesh['gx'=16,'gy'=2] {'gx','gy'}, use_global_device_ids=true, to_apply=%region_2.10 | all-reduce | flops 128 | bytes 1024 | tf_op jit(solution)/shard_map/psum | solution.py:151
  200.4 1.3 pad_maximum_fusion.1
  201.7 1.2 fusion.178
  212.8 1.6 gather_fusion.27
  224.0 1.5 gather_fusion.35
  229.2 1.4 gather_fusion.50
  230.7 1.4 gather_fusion.41
  232.1 1.6 gather_fusion.38
  238.1 1.4 gather_fusion.44
  255.6 39.6 %all-reduce.2.cloned.1.call-done = f32[27,128,128]{2,1,0:T(8,128)} async-done(((f32[27,128,128]{2,1,0:T(8,128)}), f32[27,128,128]{2,1,0:T(8,128)}) %all-reduce.2.cloned.1.call-update) | async-done | bytes 1769488 | tf_op jit(solution)/shard_map/psum | solution.py:151
  295.1 2.9 copy.308
  (476 shorter events, 152.4 us)
Async XLA Ops:
  7.2 46.1 %copy-start.1 = (bf16[1,1,2,512,128]{4,3,2,1,0:T(8,128)(2,1)S(1)}, bf16[1,1,2,512,128]{4,3,2,1,0:T(8,128)(2,1)}, u32[]{:S(2)}) copy-start(bf16[1,1,2,512,128]{4,3,2,1,0:T(8,128)(2,1)} %param.19) | copy-start | bytes 786436
  7.2 288.0 %all-reduce.2.cloned.1.call-start = ((), (), s32[]{:S(2)}) async-start(), calls=%async_computation | async-start | bytes 3538944 | tf_op jit(solution)/shard_map/psum | solution.py:151
  10.1 38.4 %collective-permute-start = (bf16[1,1,2,512,128]{4,3,2,1,0:T(8,128)(2,1)S(1)}, bf16[1,1,2,512,128]{4,3,2,1,0:T(8,128)(2,1)S(1)}, u32[]{:S(2)}, u32[]{:S(2)}) collective-permute-start(bf16[1,1,2,512,128]{4,3,2,1,0:T(8,128)(2,1)S(1)} %broadcast_select_fusion.1), channel_id=1, source_target_pairs={{0,2},{2,4},{4,6},{6,8},{8,10},{10,12},{12,14},{14,16},{16,18},{18... | collective-permute-start | bytes 786440 | tf_op jit(solution)/shard_map/ppermute | solution.py:18
  15.0 33.5 %collective-permute-start.1 = (bf16[1,1,2,512,128]{4,3,2,1,0:T(8,128)(2,1)S(1)}, bf16[1,1,2,512,128]{4,3,2,1,0:T(8,128)(2,1)S(1)}, u32[]{:S(2)}, u32[]{:S(2)}) collective-permute-start(bf16[1,1,2,512,128]{4,3,2,1,0:T(8,128)(2,1)S(1)} %broadcast_select_fusion.1), channel_id=1, source_target_pairs={{2,0},{4,2},{6,4},{8,6},{10,8},{12,10},{14,12},{16,14},{18,16},{20... | collective-permute-start | bytes 786440 | tf_op jit(solution)/shard_map/ppermute | solution.py:19
  18.2 41.5 %copy-start.45 = (pred[2]{0:T(512)(128)(4,1)}, pred[2]{0:T(512)(128)(4,1)S(1)}, u32[]{:S(2)}) copy-start(pred[2]{0:T(512)(128)(4,1)S(1)} %compare_and_fusion.16) | copy-start | bytes 10
  20.7 39.1 %copy-start.33 = (pred[2]{0:T(512)(128)(4,1)}, pred[2]{0:T(512)(128)(4,1)S(1)}, u32[]{:S(2)}) copy-start(pred[2]{0:T(512)(128)(4,1)S(1)} %get-tuple-element.46) | copy-start | bytes 10
  20.7 39.8 %copy-start.31 = (pred[2]{0:T(512)(128)(4,1)}, pred[2]{0:T(512)(128)(4,1)S(1)}, u32[]{:S(2)}) copy-start(pred[2]{0:T(512)(128)(4,1)S(1)} %get-tuple-element.44) | copy-start | bytes 10
  34.7 24.5 %copy-start.20 = (s32[1024]{0:T(1024)}, s32[1024]{0:T(1024)S(1)}, u32[]{:S(2)}) copy-start(s32[1024]{0:T(1024)S(1)} %pad_clamp_fusion.16) | copy-start | bytes 12292
  34.7 25.1 %copy-start.19 = (s32[1024]{0:T(1024)}, s32[1024]{0:T(1024)S(1)}, u32[]{:S(2)}) copy-start(s32[1024]{0:T(1024)S(1)} %pad_clamp_fusion.14) | copy-start | bytes 12292
  35.3 25.2 %copy-start.18 = (s32[1024]{0:T(1024)}, s32[1024]{0:T(1024)S(1)}, u32[]{:S(2)}) copy-start(s32[1024]{0:T(1024)S(1)} %pad_clamp_fusion.11) | copy-start | bytes 12292
  48.6 4.8 %collective-permute-start.2 = (bf16[3,1,2,512,128]{4,3,2,1,0:T(8,128)(2,1)S(1)}, bf16[3,1,2,512,128]{4,3,2,1,0:T(8,128)(2,1)S(1)}, u32[]{:S(2)}, u32[]{:S(2)}) collective-permute-start(bf16[3,1,2,512,128]{4,3,2,1,0:T(8,128)(2,1)S(1)} %pad_maximum_fusion.2), channel_id=1, source_target_pairs={{0,1},{2,3},{4,5},{6,7},{8,9},{10,11},{12,13},{14,15},{16,17},{18,... | collective-permute-start | bytes 2359304 | tf_op jit(solution)/shard_map/ppermute | solution.py:18
  50.1 4.2 %collective-permute-start.3 = (bf16[3,1,2,512,128]{4,3,2,1,0:T(8,128)(2,1)S(1)}, bf16[3,1,2,512,128]{4,3,2,1,0:T(8,128)(2,1)S(1)}, u32[]{:S(2)}, u32[]{:S(2)}) collective-permute-start(bf16[3,1,2,512,128]{4,3,2,1,0:T(8,128)(2,1)S(1)} %pad_maximum_fusion.2), channel_id=1, source_target_pairs={{1,0},{3,2},{5,4},{7,6},{9,8},{11,10},{13,12},{15,14},{17,16},{19,... | collective-permute-start | bytes 2359304 | tf_op jit(solution)/shard_map/ppermute | solution.py:19
  68.3 14.4 %copy-start.38 = (pred[2]{0:T(512)(128)(4,1)S(1)}, pred[2]{0:T(512)(128)(4,1)}, u32[]{:S(2)}) copy-start(pred[2]{0:T(512)(128)(4,1)} %get-tuple-element.60) | copy-start | bytes 10
  68.4 20.6 %copy-start.12 = (bf16[18,1,1,1,128]{4,3,2,1,0:T(2,128)(2,1)S(1)}, bf16[18,1,1,1,128]{4,3,2,1,0:T(2,128)(2,1)}, u32[]{:S(2)}) copy-start(bf16[18,1,1,1,128]{4,3,2,1,0:T(2,128)(2,1)} %get-tuple-element.100) | copy-start | bytes 13828
  68.4 22.6 %copy-start.11 = (bf16[18,1,1,1,128]{4,3,2,1,0:T(2,128)(2,1)S(1)}, bf16[18,1,1,1,128]{4,3,2,1,0:T(2,128)(2,1)}, u32[]{:S(2)}) copy-start(bf16[18,1,1,1,128]{4,3,2,1,0:T(2,128)(2,1)} %get-tuple-element.98) | copy-start | bytes 13828
  122.6 25.7 %collective-permute-start.4 = (bf16[1,1,2,512,128]{4,3,2,1,0:T(8,128)(2,1)S(1)}, bf16[1,1,2,512,128]{4,3,2,1,0:T(8,128)(2,1)S(1)}, u32[]{:S(2)}, u32[]{:S(2)}) collective-permute-start(bf16[1,1,2,512,128]{4,3,2,1,0:T(8,128)(2,1)S(1)} %bitcast.836), channel_id=1, source_target_pairs={{0,2},{2,4},{4,6},{6,8},{8,10},{10,12},{12,14},{14,16},{16,18},{18... | collective-permute-start | bytes 786440 | tf_op jit(solution)/shard_map/ppermute | solution.py:18
  127.0 21.4 %collective-permute-start.5 = (bf16[1,1,2,512,128]{4,3,2,1,0:T(8,128)(2,1)S(1)}, bf16[1,1,2,512,128]{4,3,2,1,0:T(8,128)(2,1)S(1)}, u32[]{:S(2)}, u32[]{:S(2)}) collective-permute-start(bf16[1,1,2,512,128]{4,3,2,1,0:T(8,128)(2,1)S(1)} %bitcast.837), channel_id=1, source_target_pairs={{2,0},{4,2},{6,4},{8,6},{10,8},{12,10},{14,12},{16,14},{18,16},{20... | collective-permute-start | bytes 786440 | tf_op jit(solution)/shard_map/ppermute | solution.py:19
  149.3 51.1 %collective-permute-start.6 = (bf16[3,1,2,512,128]{4,3,2,1,0:T(8,128)(2,1)}, bf16[3,1,2,512,128]{4,3,2,1,0:T(8,128)(2,1)S(1)}, u32[]{:S(2)}, u32[]{:S(2)}) collective-permute-start(bf16[3,1,2,512,128]{4,3,2,1,0:T(8,128)(2,1)} %pad_maximum_fusion.3), channel_id=1, source_target_pairs={{0,1},{2,3},{4,5},{6,7},{8,9},{10,11},{12,13},{14,15},{16,17},{18,... | collective-permute-start | bytes 2359304 | tf_op jit(solution)/shard_map/ppermute | solution.py:18
  151.3 49.1 %collective-permute-start.7 = (bf16[3,1,2,512,128]{4,3,2,1,0:T(8,128)(2,1)}, bf16[3,1,2,512,128]{4,3,2,1,0:T(8,128)(2,1)}, u32[]{:S(2)}, u32[]{:S(2)}) collective-permute-start(bf16[3,1,2,512,128]{4,3,2,1,0:T(8,128)(2,1)} %pad_maximum_fusion.3), channel_id=1, source_target_pairs={{1,0},{3,2},{5,4},{7,6},{9,8},{11,10},{13,12},{15,14},{17,16},{19,... | collective-permute-start | bytes 2359304 | tf_op jit(solution)/shard_map/ppermute | solution.py:19
  207.8 10.4 %copy-start.22 = (pred[2]{0:T(512)(128)(4,1)S(1)}, pred[2]{0:T(512)(128)(4,1)}, u32[]{:S(2)}) copy-start(pred[2]{0:T(512)(128)(4,1)} %get-tuple-element.40) | copy-start | bytes 10
  220.1 6.1 %copy-start.7 = (bf16[18,1,8,1,128]{4,3,2,1,0:T(2,128)(2,1)S(1)}, bf16[18,1,8,1,128]{4,3,2,1,0:T(2,128)(2,1)}, u32[]{:S(2)}) copy-start(bf16[18,1,8,1,128]{4,3,2,1,0:T(2,128)(2,1)} %get-tuple-element.80) | copy-start | bytes 110596
  220.1 6.8 %copy-start.26 = (pred[2]{0:T(512)(128)(4,1)S(1)}, pred[2]{0:T(512)(128)(4,1)}, u32[]{:S(2)}) copy-start(pred[2]{0:T(512)(128)(4,1)} %get-tuple-element.34) | copy-start | bytes 10
  220.1 6.8 %copy-start.27 = (pred[2]{0:T(512)(128)(4,1)S(1)}, pred[2]{0:T(512)(128)(4,1)}, u32[]{:S(2)}) copy-start(pred[2]{0:T(512)(128)(4,1)} %get-tuple-element.36) | copy-start | bytes 10
  220.1 6.8 %copy-start.42 = (pred[2]{0:T(512)(128)(4,1)S(1)}, pred[2]{0:T(512)(128)(4,1)}, u32[]{:S(2)}) copy-start(pred[2]{0:T(512)(128)(4,1)} %compare_and_fusion.5) | copy-start | bytes 10
  220.1 6.8 %copy-start.49 = (pred[2]{0:T(512)(128)(4,1)S(1)}, pred[2]{0:T(512)(128)(4,1)}, u32[]{:S(2)}) copy-start(pred[2]{0:T(512)(128)(4,1)} %compare_and_fusion.3) | copy-start | bytes 10
  220.1 7.0 %copy-start.10 = (bf16[18,1,1,1,128]{4,3,2,1,0:T(2,128)(2,1)S(1)}, bf16[18,1,1,1,128]{4,3,2,1,0:T(2,128)(2,1)}, u32[]{:S(2)}) copy-start(bf16[18,1,1,1,128]{4,3,2,1,0:T(2,128)(2,1)} %get-tuple-element.69) | copy-start | bytes 13828
  220.1 7.6 %copy-start.9 = (bf16[18,1,1,1,128]{4,3,2,1,0:T(2,128)(2,1)S(1)}, bf16[18,1,1,1,128]{4,3,2,1,0:T(2,128)(2,1)}, u32[]{:S(2)}) copy-start(bf16[18,1,1,1,128]{4,3,2,1,0:T(2,128)(2,1)} %get-tuple-element.68) | copy-start | bytes 13828
  220.1 13.7 %copy-start.21 = (pred[2]{0:T(512)(128)(4,1)S(1)}, pred[2]{0:T(512)(128)(4,1)}, u32[]{:S(2)}) copy-start(pred[2]{0:T(512)(128)(4,1)} %get-tuple-element.35) | copy-start | bytes 10
  220.1 16.5 %copy-start.16 = (bf16[18,1,1,1,128]{4,3,2,1,0:T(2,128)(2,1)S(1)}, bf16[18,1,1,1,128]{4,3,2,1,0:T(2,128)(2,1)}, u32[]{:S(2)}) copy-start(bf16[18,1,1,1,128]{4,3,2,1,0:T(2,128)(2,1)} %get-tuple-element.67) | copy-start | bytes 13828
  220.1 16.5 %copy-start.17 = (bf16[18,1,1,1,128]{4,3,2,1,0:T(2,128)(2,1)S(1)}, bf16[18,1,1,1,128]{4,3,2,1,0:T(2,128)(2,1)}, u32[]{:S(2)}) copy-start(bf16[18,1,1,1,128]{4,3,2,1,0:T(2,128)(2,1)} %get-tuple-element.72) | copy-start | bytes 13828
  220.2 20.1 %copy-start.6 = (bf16[18,1,8,1,128]{4,3,2,1,0:T(2,128)(2,1)S(1)}, bf16[18,1,8,1,128]{4,3,2,1,0:T(2,128)(2,1)}, u32[]{:S(2)}) copy-start(bf16[18,1,8,1,128]{4,3,2,1,0:T(2,128)(2,1)} %get-tuple-element.82) | copy-start | bytes 110596
  220.2 24.4 %copy-start.25 = (pred[2]{0:T(512)(128)(4,1)S(1)}, pred[2]{0:T(512)(128)(4,1)}, u32[]{:S(2)}) copy-start(pred[2]{0:T(512)(128)(4,1)} %get-tuple-element.59) | copy-start | bytes 10
  (30 other events, 98.8 us)
Sparse Core Ops, SparseCore 0:
  156.3 138.7 all-reduce.1
where the time goes:
time: 307 us; the launch traced here: 305 us
  local copies, waits for them, and re-layouts  76.8 us (25%)
  other arithmetic  72.2 us (24%)
  blocking collectives  44.2 us (14%)
  waiting for transfers between devices  40.5 us (13%)
  matrix products  37.2 us (12%)
  starting transfers between devices  18.4 us (6%)
  between operations  15.7 us (5%)
    gather x52, local copies, waits for them, and re-layouts, assemble(): block_piece = jnp.take(region, jnp.maximum(slot_codes[:, k], 0), axis=0)  45.4 us
    psum x1, blocking collectives, on_device(): weight_grad, gain_grad = lax.psum((local_weight, local_gain), ('gx', 'gy'))  44.2 us
    psum x1, waiting for transfers between devices, on_device(): weight_grad, gain_grad = lax.psum((local_weight, local_gain), ('gx', 'gy'))  39.6 us
    select_n x42, other arithmetic, assemble(): jnp.where(present, block_piece, jnp.zeros((), block_piece.dtype))  25.5 us
    dot_general x27, matrix products, weight_terms(): lax.dot_general(window(padded_tile, a, b, c), scaled, (((0,), (0,)), ((),...  24.3 us
    and x26, other arithmetic, assemble(): block_piece = jnp.take(region, jnp.maximum(slot_codes[:, k], 0), axis=0)  13.8 us
    gather x26, other arithmetic  13.7 us
    ppermute x4, starting transfers between devices, padded(): before = lax.ppermute(last, axis, up)  12.8 us
  transfers between devices with their start and end apart: 9, of which 2 were waited for; matrix products, arithmetic and copies ran while one was open for 36% of the time, Pallas kernels for 0%

commit v1 on v0

v1 whole, which is shorter than its diff:
```python
from functools import partial

import jax
import jax.numpy as jnp
from jax import lax
from jax.experimental import pallas as pl
from jax.experimental.pallas import tpu as pltpu
from jax.sharding import PartitionSpec as P

MESH = pl.DeviceIdType.MESH
BF = jnp.bfloat16
F32 = jnp.float32
SIDES = [(a, b) for a in (-1, 0, 1) for b in (-1, 0, 1) if (a, b) != (0, 0)]
TILE = 16


class Plan:
    def __init__(self, gx, gy, rows):
        low = 4 if gx % 4 == 0 else 1
        groups = {"core": gy, "low": low, "high": gx // low}
        self.low = low
        unit = gx * gy * TILE
        units = -(-(rows + TILE) // unit)
        second = units * 2 // 7
        self.rows = units * unit
        self.streams = []
        slot = 0
        room = 0
        for start, count, order in (
            (0, units - second, ("core", "low", "high")),
            (units - second, second, ("core", "high", "low")),
        ):
            if count == 0:
                continue
            phases = []
            size = count * unit
            for name in order:
                g = groups[name]
                if g == 1:
                    continue
                size //= g
                phases.append(dict(name=name, g=g, n=size, slot=slot, room=room))
                slot += g - 1
                room += (g - 1) * size
            self.streams.append(dict(start=start * unit, rows=count * unit, phases=phases))
        self.slots = slot
        self.room = room
        self.groups = [(name, g) for name, g in groups.items() if g > 1]

    def rank(self, name, i, j):
        if name == "core":
            return j
        return lax.rem(i, self.low) if name == "low" else i // self.low

    def peer(self, name, i, j, q):
        if name == "core":
            return (i, q)
        if name == "low":
            return (i - lax.rem(i, self.low) + q, j)
        return (q * self.low + lax.rem(i, self.low), j)


def face(d):
    return slice(0, 8) if d == 0 else (slice(7, 8) if d > 0 else slice(0, 1))


def rim(d):
    return slice(0, 8) if d == 0 else (slice(7, 8) if d < 0 else slice(0, 1))


def kernel(plan, gx, gy, cap, C,
           codes, x_hbm, dy_hbm, w_hbm, gain_ref,
           out_ref, grad_ref, sum_hbm,
           gx_buf, gu_buf, even, odd, w_v, wt_v, dy_v, pg_v, s_v, acc, send, recv, whole,
           in_sem, xs_sem, xr_sem, us_sem, ur_sem, rs_s, rs_r, ag_s, ag_r):
    i = lax.axis_index("gx")
    j = lax.axis_index("gy")
    V = 512

    def inside(a, b):
        ok = None
        for t in ([i + a >= 0] if a < 0 else []) + ([i + a < gx] if a > 0 else []) + (
                [j + b >= 0] if b < 0 else []) + ([j + b < gy] if b > 0 else []):
            ok = t if ok is None else jnp.logical_and(ok, t)
        return ok

    own = pl.ds(4 * cap, cap)
    load_x = pltpu.make_async_copy(x_hbm, gx_buf.at[own], in_sem.at[0])
    load_w = pltpu.make_async_copy(w_hbm, w_v, in_sem.at[1])
    load_dy = pltpu.make_async_copy(dy_hbm, dy_v, in_sem.at[2])
    load_x.start()
    load_w.start()
    load_dy.start()

    barrier = pltpu.get_barrier_semaphore()
    count = jnp.int32(sum(g - 1 for _, g in plan.groups))
    for a, b in SIDES:
        ok = inside(a, b)
        count = count + ok.astype(jnp.int32)

        @pl.when(ok)
        def _():
            pl.semaphore_signal(barrier, inc=1, device_id=(i + a, j + b), device_id_type=MESH)

    for name, g in plan.groups:
        r = plan.rank(name, i, j)
        for d in range(1, g):
            pl.semaphore_signal(barrier, inc=1, device_id=plan.peer(name, i, j, lax.rem(r + d, g)),
                                device_id_type=MESH)
    pl.semaphore_wait(barrier, count)

    def halo(src, buf, ssem, rsem, m):
        a, b = SIDES[m]
        back = pl.ds((3 * (1 - a) + (1 - b)) * cap, cap)
        return pltpu.make_async_remote_copy(
            src_ref=src.at[:, face(a), face(b)], dst_ref=buf.at[back, face(a), face(b)],
            send_sem=ssem.at[m], recv_sem=rsem.at[m], device_id=(i + a, j + b), device_id_type=MESH)

    def halo_start(src, buf, ssem, rsem):
        for m, (a, b) in enumerate(SIDES):
            @pl.when(inside(a, b))
            def _():
                halo(src, buf, ssem, rsem, m).start()

    def halo_wait(src, buf, ssem, rsem):
        for m, (a, b) in enumerate(SIDES):
            @pl.when(inside(-a, -b))
            def _():
                halo(src, buf, ssem, rsem, m).wait_recv()

            @pl.when(inside(a, b))
            def _():
                halo(src, buf, ssem, rsem, m).wait_send()

    halo_start(x_hbm, gx_buf, xs_sem, xr_sem)

    load_w.wait()
    for k in range(27):
        wt_v[k] = w_v[26 - k].astype(F32).T.astype(BF)
    load_x.wait()
    load_dy.wait()
    halo_wait(x_hbm, gx_buf, xs_sem, xr_sem)

    def piece(buf, s, x, a, b, c):
        k = 9 * (a + 1) + 3 * (b + 1) + (c + 1)
        code = codes[s, k]
        if k == 13:
            value = buf[4 * cap + s, x]
        else:
            value = buf[jnp.maximum(code, 0), x, rim(b)]
        value = value.astype(F32)
        return jnp.where(jnp.full(value.shape, code, jnp.int32) >= 0, value, 0.0)

    def plane(buf, s, px, x, a):
        level = [jnp.concatenate([piece(buf, s, x, a, b, c) for b in (-1, 0, 1)], axis=0) for c in (-1, 0, 1)]
        z = lax.broadcasted_iota(jnp.int32, level[1].shape, 1)
        down = pltpu.roll(jnp.where(z == 7, level[0], level[1]), 1, 1)
        up = pltpu.roll(jnp.where(z == 0, level[2], level[1]), 7, 1)
        for c, value in enumerate((down, level[1], up)):
            lanes = slice(c * C, (c + 1) * C)
            even[s, px, :, :, lanes] = value.reshape(80, C).astype(BF).reshape(5, 16, C)
            odd[s, px, :, :, lanes] = value[1:9].reshape(64, C).astype(BF).reshape(4, 16, C)

    def build(buf):
        for s in range(cap):
            plane(buf, s, 0, 7, -1)

            @pl.loop(0, 8)
            def _(x):
                plane(buf, s, x + 1, x, 0)

            plane(buf, s, 9, 0, 1)

    def window(s, a, b):
        xs = slice(1 + a, 9 + a)
        if b == 0:
            return odd[s, xs].reshape(V, 3 * C)
        return (even[s, xs, 0:4] if b < 0 else even[s, xs, 1:5]).reshape(V, 3 * C)

    def conv(s, w):
        total = None
        for m in range(9):
            term = jnp.dot(window(s, m // 3 - 1, m % 3 - 1), w[3 * m:3 * m + 3].reshape(3 * C, C),
                           preferred_element_type=F32)
            total = term if total is None else total + term
        return total

    build(gx_buf)
    gain = gain_ref[...]
    gain_sum = jnp.zeros((1, C), F32)
    for s in range(cap):
        c_out = conv(s, w_v)
        full = jnp.full((V, C), codes[s, 13], jnp.int32) >= 0
        mx = jnp.where(full, gx_buf[4 * cap + s].astype(F32).reshape(V, C), 0.0)
        pre = mx + gain * c_out
        sig = jax.nn.sigmoid(pre)
        out_ref[s] = (pre * sig).astype(BF)
        dy = jnp.where(full, dy_v[s].astype(F32), 0.0)
        pg = dy * sig * (1.0 + pre * (1.0 - sig))
        pg_v[s] = pg
        scaled = gain * pg
        gu_buf[4 * cap + s] = scaled.reshape(8, 8, 8, C).astype(BF)
        s_v[:, s * V:(s + 1) * V] = scaled.T.astype(BF)
        gain_sum = gain_sum + jnp.sum(pg * c_out, axis=0, keepdims=True)

    u_src = gu_buf.at[own]
    halo_start(u_src, gu_buf, us_sem, ur_sem)

    for m in range(9):
        total = None
        for s in range(cap):
            term = jnp.dot(s_v[:, s * V:(s + 1) * V], window(s, m // 3 - 1, m % 3 - 1), preferred_element_type=F32)
            total = term if total is None else total + term
        rows = slice(m * 3 * C, (m + 1) * 3 * C)
        value = total.T
        acc[rows] = value
        send[rows] = value.astype(BF)
    last = 27 * C
    value = jnp.broadcast_to(gain_sum, (TILE, C))
    acc[last:last + TILE] = value
    send[last:last + TILE] = value.astype(BF)
    rest = plan.rows - last - TILE
    if rest:
        acc[last + TILE:] = jnp.zeros((rest, C), F32)
        send[last + TILE:] = jnp.zeros((rest, C), BF)

    base = [[jnp.int32(st["start"])] for st in plan.streams]

    def rows_at(offset, n):
        return pl.ds(pl.multiple_of(offset, TILE), n)

    def scatter(t, p):
        ph = plan.streams[t]["phases"][p]
        r = plan.rank(ph["name"], i, j)
        copies = []
        for d in range(1, ph["g"]):
            q = lax.rem(r + d, ph["g"])
            copies.append(pltpu.make_async_remote_copy(
                src_ref=send.at[rows_at(base[t][p] + q * ph["n"], ph["n"])],
                dst_ref=recv.at[pl.ds(ph["room"] + (d - 1) * ph["n"], ph["n"])],
                send_sem=rs_s.at[ph["slot"] + d - 1], recv_sem=rs_r.at[ph["slot"] + d - 1],
                device_id=plan.peer(ph["name"], i, j, q), device_id_type=MESH))
        for c in copies:
            c.start()
        return copies

    def gather(t, p):
        ph = plan.streams[t]["phases"][p]
        r = plan.rank(ph["name"], i, j)
        mine = rows_at(base[t][p] + r * ph["n"], ph["n"])
        copies = []
        for d in range(1, ph["g"]):
            q = lax.rem(r + d, ph["g"])
            copies.append(pltpu.make_async_remote_copy(
                src_ref=whole.at[mine], dst_ref=whole.at[mine],
                send_sem=ag_s.at[ph["slot"] + d - 1], recv_sem=ag_r.at[ph["slot"] + d - 1],
                device_id=plan.peer(ph["name"], i, j, q), device_id_type=MESH))
        for c in copies:
            c.start()
        return copies

    def reduce(t, p, copies):
        phases = plan.streams[t]["phases"]
        ph = phases[p]
        r = plan.rank(ph["name"], i, j)
        for c in copies:
            c.wait()
        here = base[t][p] + r * ph["n"]
        base[t].append(here)
        mine = rows_at(here, ph["n"])
        value = acc[mine]
        for d in range(1, ph["g"]):
            value = value + recv[pl.ds(ph["room"] + (d - 1) * ph["n"], ph["n"])].astype(F32)
        if p + 1 < len(phases):
            acc[mine] = value
            send[mine] = value.astype(BF)
        else:
            whole[mine] = value.astype(BF)

    def advance(pending, p):
        for t, st in enumerate(plan.streams):
            steps = len(st["phases"])
            if p < steps:
                reduce(t, p, pending[t])
            else:
                for c in pending[t] or ():
                    c.wait()
            if p + 1 < steps:
                pending[t] = scatter(t, p + 1)
            elif 2 * steps - p - 2 >= 0:
                pending[t] = gather(t, 2 * steps - p - 2)
            else:
                pending[t] = None

    pending = [scatter(t, 0) for t in range(len(plan.streams))]
    halo_wait(u_src, gu_buf, us_sem, ur_sem)
    build(gu_buf)
    advance(pending, 0)
    for s in range(cap):
        grad_ref[s] = (pg_v[s] + conv(s, wt_v)).astype(BF)
        if s == 0:
            advance(pending, 1)
    steps = max(len(st["phases"]) for st in plan.streams)
    for p in range(2, 2 * steps):
        advance(pending, p)
    done = pltpu.make_async_copy(whole, sum_hbm, in_sem.at[3])
    done.start()
    done.wait()


def on_device(gx, gy, features, cotangent, neighbours, weights, channel_gain):
    cap, C = features.shape[2], features.shape[-1]
    plan = Plan(gx, gy, 27 * C)
    V = 512
    hbm = pl.BlockSpec(memory_space=pl.ANY)
    vmem = pl.BlockSpec(memory_space=pltpu.VMEM)
    dma = pltpu.SemaphoreType.DMA
    out, grad, total = pl.pallas_call(
        partial(kernel, plan, gx, gy, cap, C),
        out_shape=(
            jax.ShapeDtypeStruct((cap, V, C), BF),
            jax.ShapeDtypeStruct((cap, V, C), BF),
            jax.ShapeDtypeStruct((plan.rows, C), BF),
        ),
        in_specs=[pl.BlockSpec(memory_space=pltpu.SMEM), hbm, hbm, hbm, vmem],
        out_specs=(vmem, vmem, hbm),
        scratch_shapes=[
            pltpu.VMEM((9 * cap, 8, 8, 8, C), BF),
            pltpu.VMEM((9 * cap, 8, 8, 8, C), BF),
            pltpu.VMEM((cap, 10, 5, 16, 3 * C), BF),
            pltpu.VMEM((cap, 10, 4, 16, 3 * C), BF),
            pltpu.VMEM((27, C, C), BF),
            pltpu.VMEM((27, C, C), BF),
            pltpu.VMEM((cap, V, C), BF),
            pltpu.VMEM((cap, V, C), F32),
            pltpu.VMEM((C, cap * V), BF),
            pltpu.VMEM((plan.rows, C), F32),
            pltpu.VMEM((plan.rows, C), BF),
            pltpu.VMEM((plan.room, C), BF),
            pltpu.VMEM((plan.rows, C), BF),
            dma((4,)), dma((8,)), dma((8,)), dma((8,)), dma((8,)),
            dma((plan.slots,)), dma((plan.slots,)), dma((plan.slots,)), dma((plan.slots,)),
        ],
        compiler_params=pltpu.CompilerParams(
            collective_id=0, has_side_effects=True, vmem_limit_bytes=60 * 1024 * 1024),
    )(
        neighbours.reshape(cap, 27),
        features.reshape(cap, 8, 8, 8, C),
        cotangent.reshape(cap, V, C),
        weights,
        channel_gain.reshape(1, C),
    )
    shape = (1, 1, cap, V, C)
    weight_grad = total[: 27 * C].astype(F32).reshape(27, C, C)
    gain_grad = total[27 * C].astype(F32)
    return out.reshape(shape), grad.reshape(shape), weight_grad, gain_grad


def solution(mesh):
    spec = P("gx", "gy", None, None, None)
    return jax.shard_map(
        partial(on_device, mesh.shape["gx"], mesh.shape["gy"]),
        mesh=mesh,
        in_specs=(spec, spec, P("gx", "gy", None, None), P(), P()),
        out_specs=(spec, spec, P(), P()),
        check_vma=False,
    )
```

time: 307 us -> 46 us (0.15)
  local copies, waits for them, and re-layouts: 76.8 us -> 2.64 us
  other arithmetic: 72.2 us -> 2.59 us
  blocking collectives: 44.2 us -> 0 us
  waiting for transfers between devices: 40.5 us -> 0 us
  Pallas kernels: 0 us -> 39.9 us
  matrix products: 37.2 us -> 0 us
  starting transfers between devices: 18.4 us -> 0 us
  between operations: 15.7 us -> 0.66 us
    gather x52 -> x0, local copies, waits for them, and re-layouts: 45.4 us -> none  [assemble(): block_piece = jnp.take(region, jnp.maximum(slot_codes[:, k], 0), axis=0)]
    psum x1 -> x0, blocking collectives: 44.2 us -> none  [on_device(): weight_grad, gain_grad = lax.psum((local_weight, local_gain), ('gx', 'gy'))]
    pallas_call x0 -> x1, Pallas kernels: none -> 39.9 us  [on_device(): pl.pallas_call(partial(kernel, plan, gx, gy, cap, C), out_shape=(jax.Shap...]
    psum x1 -> x0, waiting for transfers between devices: 39.6 us -> none  [on_device(): weight_grad, gain_grad = lax.psum((local_weight, local_gain), ('gx', 'gy'))]
    dot_general x81 -> x0, matrix products: 37.2 us -> none  [the longest x27 24.3 us: weight_terms(): lax.dot_general(window(padded_tile, a, b, c), scaled, (((0,), (0,)), ((),...]
    select_n x70 -> x0, other arithmetic: 26.7 us -> none  [the longest x42 25.5 us: assemble(): jnp.where(present, block_piece, jnp.zeros((), block_piece.dtype))]
    ppermute x8 -> x0, starting transfers between devices: 18.3 us -> none  [the longest x4 12.8 us: padded(): before = lax.ppermute(last, axis, up)]
    and x26 -> x0, other arithmetic: 13.8 us -> none  [assemble(): block_piece = jnp.take(region, jnp.maximum(slot_codes[:, k], 0), axis=0)]
  transfers between devices with their start and end apart: 9 -> 0, of which waited for: 2 -> 0; matrix products, arithmetic and copies ran while one was open for 36% -> 0% of each run, Pallas kernels for 0% -> 0%
where the time goes in v1:
time: 46 us; the launch traced here: 45.8 us
  Pallas kernels  39.9 us (87%)
  local copies, waits for them, and re-layouts  2.64 us (6%)
  other arithmetic  2.59 us (6%)
  between operations  0.66 us (1%)
    pallas_call x1, Pallas kernels, on_device(): pl.pallas_call(partial(kernel, plan, gx, gy, cap, C), out_shape=(jax.Shap...  39.9 us
    unnamed x6, local copies, waits for them, and re-layouts  1.41 us
    reshape x1, other arithmetic, on_device(): weight_grad = total[:27 * C].astype(F32).reshape(27, C, C)  1.41 us
    slice x1, local copies, waits for them, and re-layouts, on_device(): weight_grad = total[:27 * C].astype(F32).reshape(27, C, C)  1.22 us
    convert_element_type x1, other arithmetic, on_device(): gain_grad = total[27 * C].astype(F32)  1.19 us

profile of v1, /device:TPU:0, one launch (start us, length us, event | category | flops | bytes accessed | tf_op | source)
XLA Modules:
  0.0 45.8 jit_solution(15193968120904803170)
XLA Ops:
  0.6 39.9 %shard_map.84 = (bf16[2,512,128]{2,1,0:T(8,128)(2,1)}, bf16[2,512,128]{2,1,0:T(8,128)(2,1)}, bf16[3584,128]{1,0:T(8,128)(2,1)}) custom-call(s32[2,27]{1,0:T(2,128)} %bitcast.16, bf16[2,8,8,8,128]{4,3,2,1,0:T(8,128)(2,1)} %bitcast.14, bf16[2,512,128]{2,1,0:T(8,128)(2,1)} %bitcast.15, bf16[27,128,128]{2,1,0:T(8,128)(2,1)} %w_hbm.1, f32[1,128]{1,0:T(1,128)} %bitcast.17), custom_call_target="tpu_custom_call" | custom-call | tf_op jit(solution)/shard_map/pallas_call | solution.py:318
  40.5 1.2 %bitcast_convert_fusion = f32[128]{0:T(128)} fusion(bf16[3584,128]{1,0:T(8,128)(2,1)} %get-tuple-element.9), kind=kLoop, calls=%fused_computation | loop fusion | flops 128 | bytes 768 | tf_op jit(solution)/shard_map/convert_element_type | solution.py:355
  41.7 1.2 %slice.6 = bf16[3456,128]{1,0:T(8,128)(2,1)S(1)} slice(bf16[3584,128]{1,0:T(8,128)(2,1)} %get-tuple-element.9), slice={[0:3456], [0:128]} | slice | bytes 1769472 | tf_op jit(solution)/shard_map/slice | solution.py:354
  42.9 0.0 copy-start.1
  42.9 0.0 copy-start
  42.9 1.4 %convert.2 = f32[27,128,128]{2,1,0:T(8,128)} convert(bf16[27,128,128]{2,1,0:T(8,128)(2,1)S(1)} %bitcast.11) | non-fusion elementwise | flops 442368 | bytes 2654208 | tf_op jit(solution)/shard_map/reshape | solution.py:354
  44.3 0.0 copy-done.1
  44.4 0.7 %copy.11 = bf16[1,1,2,512,128]{4,3,2,1,0:T(8,128)(2,1)} copy(bf16[1,1,2,512,128]{4,3,2,1,0:T(8,128)(2,1)S(1)} %bitcast.13) | data formatting | bytes 524288
  45.1 0.0 copy-done
  45.1 0.7 %copy.12 = bf16[1,1,2,512,128]{4,3,2,1,0:T(8,128)(2,1)} copy(bf16[1,1,2,512,128]{4,3,2,1,0:T(8,128)(2,1)S(1)} %bitcast.12) | data formatting | bytes 524288
Async XLA Ops:
  42.9 1.4 %copy-start.1 = (bf16[2,512,128]{2,1,0:T(8,128)(2,1)S(1)}, bf16[2,512,128]{2,1,0:T(8,128)(2,1)}, u32[]{:S(2)}) copy-start(bf16[2,512,128]{2,1,0:T(8,128)(2,1)} %get-tuple-element.7) | copy-start | bytes 786436
  42.9 2.1 %copy-start = (bf16[2,512,128]{2,1,0:T(8,128)(2,1)S(1)}, bf16[2,512,128]{2,1,0:T(8,128)(2,1)}, u32[]{:S(2)}) copy-start(bf16[2,512,128]{2,1,0:T(8,128)(2,1)} %get-tuple-element.8) | copy-start | bytes 786436

commit v2 on v1

--- a/solution.py
+++ b/solution.py
@@ -20,7 +20,7 @@
         groups = {"core": gy, "low": low, "high": gx // low}
         self.low = low
         unit = gx * gy * TILE
-        units = -(-(rows + TILE) // unit)
+        units = -(-rows // unit)
         second = units * 2 // 7
         self.rows = units * unit
         self.streams = []
@@ -46,6 +46,7 @@
         self.slots = slot
         self.room = room
         self.groups = [(name, g) for name, g in groups.items() if g > 1]
+        self.members = sum(g for _, g in self.groups)
 
     def rank(self, name, i, j):
         if name == "core":
@@ -70,9 +71,9 @@
 
 def kernel(plan, gx, gy, cap, C,
            codes, x_hbm, dy_hbm, w_hbm, gain_ref,
-           out_ref, grad_ref, sum_hbm,
-           gx_buf, gu_buf, even, odd, w_v, wt_v, dy_v, pg_v, s_v, acc, send, recv, whole,
-           in_sem, xs_sem, xr_sem, us_sem, ur_sem, rs_s, rs_r, ag_s, ag_r):
+           out_ref, grad_ref, sum_ref, gsum_ref,
+           gx_buf, gu_buf, even, odd, w_v, wt_v, dy_v, pg_v, s_v, acc, send, recv, whole, gbuf,
+           in_sem, xs_sem, xr_sem, us_sem, ur_sem, rs_s, rs_r, ag_s, ag_r, g_s, g_r):
     i = lax.axis_index("gx")
     j = lax.axis_index("gy")
     V = 512
@@ -216,13 +217,10 @@
         acc[rows] = value
         send[rows] = value.astype(BF)
     last = 27 * C
-    value = jnp.broadcast_to(gain_sum, (TILE, C))
-    acc[last:last + TILE] = value
-    send[last:last + TILE] = value.astype(BF)
-    rest = plan.rows - last - TILE
+    rest = plan.rows - last
     if rest:
-        acc[last + TILE:] = jnp.zeros((rest, C), F32)
-        send[last + TILE:] = jnp.zeros((rest, C), BF)
+        acc[last:] = jnp.zeros((rest, C), F32)
+        send[last:] = jnp.zeros((rest, C), BF)
 
     base = [[jnp.int32(st["start"])] for st in plan.streams]
 
@@ -292,20 +290,67 @@
             else:
                 pending[t] = None
 
+    starts = [sum(g for _, g in plan.groups[:h]) for h in range(len(plan.groups))]
+
+    def gain_send(h, value):
+        name, g = plan.groups[h]
+        r = plan.rank(name, i, j)
+        gbuf[starts[h] + r] = jnp.broadcast_to(value, (8, C))
+        copies = []
+        for d in range(1, g):
+            copies.append(pltpu.make_async_remote_copy(
+                src_ref=gbuf.at[starts[h] + r], dst_ref=gbuf.at[starts[h] + r],
+                send_sem=g_s.at[starts[h] + d], recv_sem=g_r.at[starts[h] + d],
+                device_id=plan.peer(name, i, j, lax.rem(r + d, g)), device_id_type=MESH))
+        for c in copies:
+            c.start()
+        return copies
+
+    def gain_sum_of(h, copies):
+        for c in copies:
+            c.wait()
+        value = gbuf[starts[h]]
+        for q in range(1, plan.groups[h][1]):
+            value = value + gbuf[starts[h] + q]
+        return value
+
     pending = [scatter(t, 0) for t in range(len(plan.streams))]
+    value = gain_sum
+    flight = gain_send(0, value) if plan.groups else None
+    advance(pending, 0)
+    for h in range(1, len(plan.groups)):
+        if h == 1:
+            value = gain_sum_of(0, flight)
+            flight = gain_send(1, value)
     halo_wait(u_src, gu_buf, us_sem, ur_sem)
     build(gu_buf)
-    advance(pending, 0)
     for s in range(cap):
         grad_ref[s] = (pg_v[s] + conv(s, wt_v)).astype(BF)
-        if s == 0:
-            advance(pending, 1)
     steps = max(len(st["phases"]) for st in plan.streams)
-    for p in range(2, 2 * steps):
+    for p in range(1, 2 * steps):
         advance(pending, p)
-    done = pltpu.make_async_copy(whole, sum_hbm, in_sem.at[3])
-    done.start()
-    done.wait()
+        if p < len(plan.groups):
+            value = gain_sum_of(p, flight)
+            if p + 1 < len(plan.groups):
+                flight = gain_send(p + 1, value)
+    gsum_ref[...] = value
+    sum_ref[...] = whole[0:27 * C]
+
+
+def finish(out_ref, grad_ref, sum_ref, gsum_ref, out_hbm, grad_hbm, sum_hbm, gsum_out, wide, sems):
+    copies = [pltpu.make_async_copy(out_ref, out_hbm, sems.at[0]),
+              pltpu.make_async_copy(grad_ref, grad_hbm, sems.at[1])]
+    for c in copies:
+        c.start()
+    n = wide.shape[0] // 9
+    for m in range(9):
+        rows = pl.ds(m * n, n)
+        wide[rows] = sum_ref[rows].astype(F32)
+        copies.append(pltpu.make_async_copy(wide.at[rows], sum_hbm.at[rows], sems.at[2 + m]))
+        copies[-1].start()
+    gsum_out[...] = gsum_ref[0:1]
+    for c in copies:
+        c.wait()
 
 
 def on_device(gx, gy, features, cotangent, neighbours, weights, channel_gain):
@@ -313,17 +358,19 @@
     plan = Plan(gx, gy, 27 * C)
     V = 512
     hbm = pl.BlockSpec(memory_space=pl.ANY)
+    far = pl.BlockSpec(memory_space=pltpu.HBM)
     vmem = pl.BlockSpec(memory_space=pltpu.VMEM)
     dma = pltpu.SemaphoreType.DMA
-    out, grad, total = pl.pallas_call(
+    parts = pl.pallas_call(
         partial(kernel, plan, gx, gy, cap, C),
         out_shape=(
-            jax.ShapeDtypeStruct((cap, V, C), BF),
-            jax.ShapeDtypeStruct((cap, V, C), BF),
-            jax.ShapeDtypeStruct((plan.rows, C), BF),
+            pltpu.VMEM((cap, V, C), BF),
+            pltpu.VMEM((cap, V, C), BF),
+            pltpu.VMEM((27 * C, C), BF),
+            pltpu.VMEM((8, C), F32),
         ),
-        in_specs=[pl.BlockSpec(memory_space=pltpu.SMEM), hbm, hbm, hbm, vmem],
-        out_specs=(vmem, vmem, hbm),
+        in_specs=[pl.BlockSpec(memory_space=pltpu.SMEM), far, far, far, vmem],
+        out_specs=(vmem, vmem, vmem, vmem),
         scratch_shapes=[
             pltpu.VMEM((9 * cap, 8, 8, 8, C), BF),
             pltpu.VMEM((9 * cap, 8, 8, 8, C), BF),
@@ -338,11 +385,13 @@
             pltpu.VMEM((plan.rows, C), BF),
             pltpu.VMEM((plan.room, C), BF),
             pltpu.VMEM((plan.rows, C), BF),
-            dma((4,)), dma((8,)), dma((8,)), dma((8,)), dma((8,)),
+            pltpu.VMEM((plan.members, 8, C), F32),
+            dma((3,)), dma((8,)), dma((8,)), dma((8,)), dma((8,)),
             dma((plan.slots,)), dma((plan.slots,)), dma((plan.slots,)), dma((plan.slots,)),
+            dma((plan.members,)), dma((plan.members,)),
         ],
         compiler_params=pltpu.CompilerParams(
-            collective_id=0, has_side_effects=True, vmem_limit_bytes=60 * 1024 * 1024),
+            collective_id=0, has_side_effects=True, vmem_limit_bytes=62 * 1024 * 1024),
     )(
         neighbours.reshape(cap, 27),
         features.reshape(cap, 8, 8, 8, C),
@@ -351,9 +400,20 @@
         channel_gain.reshape(1, C),
     )
     shape = (1, 1, cap, V, C)
-    weight_grad = total[: 27 * C].astype(F32).reshape(27, C, C)
-    gain_grad = total[27 * C].astype(F32)
-    return out.reshape(shape), grad.reshape(shape), weight_grad, gain_grad
+    out, grad, weight_grad, gain_grad = pl.pallas_call(
+        finish,
+        out_shape=(
+            jax.ShapeDtypeStruct((cap, V, C), BF),
+            jax.ShapeDtypeStruct((cap, V, C), BF),
+            jax.ShapeDtypeStruct((27 * C, C), F32),
+            jax.ShapeDtypeStruct((1, C), F32),
+        ),
+        in_specs=[vmem] * 4,
+        out_specs=(hbm, hbm, hbm, vmem),
+        scratch_shapes=[pltpu.VMEM((27 * C, C), F32), dma((11,))],
+        compiler_params=pltpu.CompilerParams(vmem_limit_bytes=16 * 1024 * 1024),
+    )(*parts)
+    return out.reshape(shape), grad.reshape(shape), weight_grad.reshape(27, C, C), gain_grad.reshape(C)
 
 
 def solution(mesh):

time: 46 us -> 39.8 us (0.87)
  local copies, waits for them, and re-layouts: 2.64 us -> 0 us
  other arithmetic: 2.59 us -> 0 us
  Pallas kernels: 39.9 us -> 38.9 us
    unnamed x6 -> x0, local copies, waits for them, and re-layouts: 1.41 us -> none
    reshape x1 -> x0, other arithmetic: 1.41 us -> none  [on_device(): weight_grad = total[:27 * C].astype(F32).reshape(27, C, C)]
    slice x1 -> x0, local copies, waits for them, and re-layouts: 1.22 us -> none  [on_device(): weight_grad = total[:27 * C].astype(F32).reshape(27, C, C)]
    convert_element_type x1 -> x0, other arithmetic: 1.19 us -> none  [on_device(): gain_grad = total[27 * C].astype(F32)]
    pallas_call x1 -> x2, Pallas kernels: 39.9 us -> 38.9 us  [the longest x1 37 us: on_device(): pl.pallas_call(partial(kernel, plan, gx, gy, cap, C), out_shape=(pltpu.VM...]
where the time goes in v2:
time: 39.8 us; the launch traced here: 39.6 us
  Pallas kernels  38.9 us (98%)
  between operations  0.64 us (2%)
    pallas_call x1, Pallas kernels, on_device(): pl.pallas_call(partial(kernel, plan, gx, gy, cap, C), out_shape=(pltpu.VM...  37 us
    pallas_call x1, Pallas kernels, on_device(): pl.pallas_call(finish, out_shape=(jax.ShapeDtypeStruct((cap, V, C), BF),...  1.97 us

profile of v2, /device:TPU:0, one launch (start us, length us, event | category | flops | bytes accessed | tf_op | source)
XLA Modules:
  0.0 39.6 jit_solution(10036529378706574801)
XLA Ops:
  0.6 37.0 %shard_map.84 = (bf16[2,512,128]{2,1,0:T(8,128)(2,1)S(1)}, bf16[2,512,128]{2,1,0:T(8,128)(2,1)S(1)}, bf16[3456,128]{1,0:T(8,128)(2,1)S(1)}, f32[8,128]{1,0:T(8,128)S(1)}) custom-call(s32[2,27]{1,0:T(2,128)} %bitcast.10, bf16[2,8,8,8,128]{4,3,2,1,0:T(8,128)(2,1)} %bitcast.8, bf16[2,512,128]{2,1,0:T(8,128)(2,1)} %bitcast.9, bf16[27,128,128]{2,1,0:T(8,128)(2,1)} %w_hbm.1, ...), custom_call_target="tpu_custom_call" | custom-call | tf_op jit(solution)/shard_map/pallas_call | solution.py:364
  37.6 2.0 %shard_map.85 = (bf16[2,512,128]{2,1,0:T(8,128)(2,1)}, bf16[2,512,128]{2,1,0:T(8,128)(2,1)}, f32[3456,128]{1,0:T(8,128)}, f32[1,128]{1,0:T(1,128)}) custom-call(bf16[2,512,128]{2,1,0:T(8,128)(2,1)S(1)} %get-tuple-element.12.out_ref, bf16[2,512,128]{2,1,0:T(8,128)(2,1)S(1)} %get-tuple-element.13.grad_ref, bf16[3456,128]{1,0:T(8,128)(2,1)S(1)} %get-tuple-element.14.sum_ref, ...), custom_call_target="tpu_custom_call" | custom-call | tf_op jit(solution)/shard_map/pallas_call | solution.py:403

commit v3 on v2

--- a/solution.py
+++ b/solution.py
@@ -10,6 +10,8 @@
 MESH = pl.DeviceIdType.MESH
 BF = jnp.bfloat16
 F32 = jnp.float32
+ORDERS = (("core", "low", "high"), ("core", "low", "high"), ("core", "high", "low"))
+CUTS = (0, 3, 5, 7)
 SIDES = [(a, b) for a in (-1, 0, 1) for b in (-1, 0, 1) if (a, b) != (0, 0)]
 TILE = 16
 
@@ -21,15 +23,13 @@
         self.low = low
         unit = gx * gy * TILE
         units = -(-rows // unit)
-        second = units * 2 // 7
+        cuts = [units * part // 7 for part in CUTS]
         self.rows = units * unit
         self.streams = []
         slot = 0
         room = 0
-        for start, count, order in (
-            (0, units - second, ("core", "low", "high")),
-            (units - second, second, ("core", "high", "low")),
-        ):
+        for start, stop, order in zip(cuts[:-1], cuts[1:], ORDERS):
+            count = stop - start
             if count == 0:
                 continue
             phases = []
@@ -207,15 +207,6 @@
     u_src = gu_buf.at[own]
     halo_start(u_src, gu_buf, us_sem, ur_sem)
 
-    for m in range(9):
-        total = None
-        for s in range(cap):
-            term = jnp.dot(s_v[:, s * V:(s + 1) * V], window(s, m // 3 - 1, m % 3 - 1), preferred_element_type=F32)
-            total = term if total is None else total + term
-        rows = slice(m * 3 * C, (m + 1) * 3 * C)
-        value = total.T
-        acc[rows] = value
-        send[rows] = value.astype(BF)
     last = 27 * C
     rest = plan.rows - last
     if rest:
@@ -314,7 +305,20 @@
             value = value + gbuf[starts[h] + q]
         return value
 
-    pending = [scatter(t, 0) for t in range(len(plan.streams))]
+    pending = [None] * len(plan.streams)
+    for m in range(9):
+        total = None
+        for s in range(cap):
+            term = jnp.dot(s_v[:, s * V:(s + 1) * V], window(s, m // 3 - 1, m % 3 - 1), preferred_element_type=F32)
+            total = term if total is None else total + term
+        rows = slice(m * 3 * C, (m + 1) * 3 * C)
+        value = total.T
+        acc[rows] = value
+        send[rows] = value.astype(BF)
+        for t, st in enumerate(plan.streams):
+            stop = st["start"] + st["rows"]
+            if pending[t] is None and (stop <= (m + 1) * 3 * C or m == 8):
+                pending[t] = scatter(t, 0)
     value = gain_sum
     flight = gain_send(0, value) if plan.groups else None
     advance(pending, 0)

time: 39.8 us -> 38.3 us (0.962)
  Pallas kernels: 38.9 us -> 37.5 us
    pallas_call x1, Pallas kernels: 37 us -> 35.5 us  [on_device(): pl.pallas_call(partial(kernel, plan, gx, gy, cap, C), out_shape=(pltpu.VM...]
where the time goes in v3:
time: 38.3 us; the launch traced here: 38.1 us
  Pallas kernels  37.5 us (98%)
  between operations  0.64 us (2%)
    pallas_call x1, Pallas kernels, on_device(): pl.pallas_call(partial(kernel, plan, gx, gy, cap, C), out_shape=(pltpu.VM...  35.5 us
    pallas_call x1, Pallas kernels, on_device(): pl.pallas_call(finish, out_shape=(jax.ShapeDtypeStruct((cap, V, C), BF),...  1.97 us

profile of v3, /device:TPU:0, one launch (start us, length us, event | category | flops | bytes accessed | tf_op | source)
XLA Modules:
  0.0 38.1 jit_solution(6413014121958892614)
XLA Ops:
  0.6 35.5 %shard_map.84 = (bf16[2,512,128]{2,1,0:T(8,128)(2,1)S(1)}, bf16[2,512,128]{2,1,0:T(8,128)(2,1)S(1)}, bf16[3456,128]{1,0:T(8,128)(2,1)S(1)}, f32[8,128]{1,0:T(8,128)S(1)}) custom-call(s32[2,27]{1,0:T(2,128)} %bitcast.10, bf16[2,8,8,8,128]{4,3,2,1,0:T(8,128)(2,1)} %bitcast.8, bf16[2,512,128]{2,1,0:T(8,128)(2,1)} %bitcast.9, bf16[27,128,128]{2,1,0:T(8,128)(2,1)} %w_hbm.1, ...), custom_call_target="tpu_custom_call" | custom-call | tf_op jit(solution)/shard_map/pallas_call | solution.py:368
  36.1 2.0 %shard_map.85 = (bf16[2,512,128]{2,1,0:T(8,128)(2,1)}, bf16[2,512,128]{2,1,0:T(8,128)(2,1)}, f32[3456,128]{1,0:T(8,128)}, f32[1,128]{1,0:T(1,128)}) custom-call(bf16[2,512,128]{2,1,0:T(8,128)(2,1)S(1)} %get-tuple-element.12.out_ref, bf16[2,512,128]{2,1,0:T(8,128)(2,1)S(1)} %get-tuple-element.13.grad_ref, bf16[3456,128]{1,0:T(8,128)(2,1)S(1)} %get-tuple-element.14.sum_ref, ...), custom_call_target="tpu_custom_call" | custom-call | tf_op jit(solution)/shard_map/pallas_call | solution.py:407

commit v4 on v3

--- a/solution.py
+++ b/solution.py
@@ -10,8 +10,8 @@
 MESH = pl.DeviceIdType.MESH
 BF = jnp.bfloat16
 F32 = jnp.float32
-ORDERS = (("core", "low", "high"), ("core", "low", "high"), ("core", "high", "low"))
-CUTS = (0, 3, 5, 7)
+ORDERS = (("core", "low", "high"), ("core", "low", "high"), ("core", "high", "low"), ("core", "high", "low"))
+CUTS = (0, 3, 5, 6, 7)
 SIDES = [(a, b) for a in (-1, 0, 1) for b in (-1, 0, 1) if (a, b) != (0, 0)]
 TILE = 16
 

time: 38.3 us -> 38.3 us (level)
  no operation moved by 1% of the time
where the time goes in v4:
time: 38.3 us; the launch traced here: 38.2 us
  Pallas kernels  37.5 us (98%)
  between operations  0.64 us (2%)
    pallas_call x1, Pallas kernels, on_device(): pl.pallas_call(partial(kernel, plan, gx, gy, cap, C), out_shape=(pltpu.VM...  35.5 us
    pallas_call x1, Pallas kernels, on_device(): pl.pallas_call(finish, out_shape=(jax.ShapeDtypeStruct((cap, V, C), BF),...  1.97 us

profile of v4, /device:TPU:0, one launch (start us, length us, event | category | flops | bytes accessed | tf_op | source)
XLA Modules:
  0.0 38.2 jit_solution(11236974299291533984)
XLA Ops:
  0.6 35.5 %shard_map.84 = (bf16[2,512,128]{2,1,0:T(8,128)(2,1)S(1)}, bf16[2,512,128]{2,1,0:T(8,128)(2,1)S(1)}, bf16[3456,128]{1,0:T(8,128)(2,1)S(1)}, f32[8,128]{1,0:T(8,128)S(1)}) custom-call(s32[2,27]{1,0:T(2,128)} %bitcast.10, bf16[2,8,8,8,128]{4,3,2,1,0:T(8,128)(2,1)} %bitcast.8, bf16[2,512,128]{2,1,0:T(8,128)(2,1)} %bitcast.9, bf16[27,128,128]{2,1,0:T(8,128)(2,1)} %w_hbm.1, ...), custom_call_target="tpu_custom_call" | custom-call | tf_op jit(solution)/shard_map/pallas_call | solution.py:368
  36.2 2.0 %shard_map.85 = (bf16[2,512,128]{2,1,0:T(8,128)(2,1)}, bf16[2,512,128]{2,1,0:T(8,128)(2,1)}, f32[3456,128]{1,0:T(8,128)}, f32[1,128]{1,0:T(1,128)}) custom-call(bf16[2,512,128]{2,1,0:T(8,128)(2,1)S(1)} %get-tuple-element.12.out_ref, bf16[2,512,128]{2,1,0:T(8,128)(2,1)S(1)} %get-tuple-element.13.grad_ref, bf16[3456,128]{1,0:T(8,128)(2,1)S(1)} %get-tuple-element.14.sum_ref, ...), custom_call_target="tpu_custom_call" | custom-call | tf_op jit(solution)/shard_map/pallas_call | solution.py:407
